TPU v7x, 32 devices: a whole 2x2x4 slice. The times are simulated.
32 devices in a mesh: rep: 4 (over x, core), shard: 8 (over z, y).
Axes of the slice: x: 2, y: 2, z: 4, core: 2. Of those that a mesh axis runs over, the one named last changes fastest.
Arguments:
- layer_input: bfloat16 [32, 1024, 768], P(('rep', 'shard')), may hold values from -6 to 6
- in_weight: bfloat16 [768, 2304], P('shard'), may hold values from -0.21875 to 0.21875
- query_bias: bfloat16 [768], P('shard'), may hold values from -4 to 4
- value_bias: bfloat16 [768], P('shard'), may hold values from -1.5 to 1.5
- out_weight: bfloat16 [768, 768], P('shard'), may hold values from -0.875 to 0.875
- out_bias: bfloat16 [768], P('shard'), may hold values from -3 to 3
- first_gain: bfloat16 [768], P('shard'), may hold values from 0.5 to 1.5
- first_shift: bfloat16 [768], P('shard'), may hold values from -3 to 3
- inner_weight: bfloat16 [768, 3072], P('shard'), may hold values from -0.21875 to 0.21875
- inner_bias: bfloat16 [3072], P('shard'), may hold values from -4 to 4
- outer_weight: bfloat16 [3072, 768], P('shard'), may hold values from -0.15625 to 0.15625
- outer_bias: bfloat16 [768], P('shard'), may hold values from -3 to 3
- second_gain: bfloat16 [768], P('shard'), may hold values from 0.5 to 1.5
- second_shift: bfloat16 [768], P('shard'), may hold values from -3 to 3
- segment_ids: int32 [32, 1024], P(('rep', 'shard')), may hold values from 0 to 3, never falling along the last dimension, each value on 1 to 512 neighbouring positions
- token_valid: int32 [32, 1024], P(('rep', 'shard')), may hold values from 0 to 1, as said below
- query_perm: int32 [32, 12, 1024], P(('rep', 'shard')), may hold values from 0 to 1023, each once within a row
- key_perm: int32 [32, 12, 1024], P(('rep', 'shard')), may hold values from 0 to 1023, each once within a row
- out_cotangent: bfloat16 [32, 1024, 768], P(('rep', 'shard')), may hold values from -6 to 6
Outputs:
- hidden_out: bfloat16 [32, 1024, 768], P(('rep', 'shard'))
- input_grad: bfloat16 [32, 1024, 768], P(('rep', 'shard'))
- grad_in_weight: float32 [768, 2304], P('shard')
- grad_query_bias: float32 [768], P('shard')
- grad_value_bias: float32 [768], P('shard')
- grad_out_weight: float32 [768, 768], P('shard')
- grad_out_bias: float32 [768], P('shard')
- grad_first_gain: float32 [768], P('shard')
- grad_first_shift: float32 [768], P('shard')
- grad_inner_weight: float32 [768, 3072], P('shard')
- grad_inner_bias: float32 [3072], P('shard')
- grad_outer_weight: float32 [3072, 768], P('shard')
- grad_outer_bias: float32 [768], P('shard')
- grad_second_gain: float32 [768], P('shard')
- grad_second_shift: float32 [768], P('shard')
Inputs may be any that keep to these rules, and one draw needn't show every extreme that they name: `token_valid`: in each sequence the real tokens come first and at least one last position is padding (0), at most 128 positions. `segment_ids`: numbers never fall along a sequence. `query_perm`: for each sequence and head, a permutation of the positions. `key_perm`: for each sequence and head, a permutation of the positions.
All inputs are finite; a program needn't handle non-finite values.
Results may differ from a plain program's by a relative error of at most 0.015.
Values may be sent and summed in bfloat16 or wider, within the bound.
A program may use at most 256 MiB of HBM per device.

v0:
```python
from functools import partial
import jax
import jax.numpy as jnp
from jax import lax
from jax.sharding import PartitionSpec as P

CL = 128
EPS = 1e-06


def norm_parts(resid):
    average = jnp.mean(resid, axis=-1, keepdims=True)
    centred = resid - average
    variance = jnp.mean(centred * centred, axis=-1, keepdims=True)
    inv_std = lax.rsqrt(variance + EPS)
    return (centred * inv_std, inv_std)


def norm_back(grad_out, normed, inv_std, gain):
    scaled = grad_out * gain
    first_term = jnp.mean(scaled, axis=-1, keepdims=True)
    second_term = jnp.mean(scaled * normed, axis=-1, keepdims=True)
    grad_in = inv_std * (scaled - first_term - normed * second_term)
    return (grad_in, jnp.sum(grad_out * normed, axis=0), jnp.sum(grad_out, axis=0))


def invert_order(order):

    def single(row_order):
        return (
            jnp.zeros_like(row_order)
            .at[row_order]
            .set(jnp.arange(row_order.shape[0], dtype=jnp.int32))
        )

    return jax.vmap(jax.vmap(single))(order)


def to_heads(tensor, seqs, heads):
    tokens, width = tensor.shape
    return jnp.transpose(tensor.reshape(seqs, tokens // seqs, heads, width // heads), (0, 2, 1, 3))


def from_heads(tensor):
    seqs, heads, length, head_size = tensor.shape
    return jnp.transpose(tensor, (0, 2, 1, 3)).reshape(seqs * length, heads * head_size)


def arrange(tensor, order):
    return jnp.take_along_axis(tensor, order[..., None], axis=2)


def in_clusters(tensor):
    seqs, heads, length, inner_dim = tensor.shape
    return tensor.reshape(seqs, heads, length // CL, CL, inner_dim)


def shards(
    layer_input,
    in_weight,
    query_bias,
    value_bias,
    out_weight,
    out_bias,
    first_gain,
    first_shift,
    inner_weight,
    inner_bias,
    outer_weight,
    outer_bias,
    second_gain,
    second_shift,
    segment_ids,
    token_valid,
    query_perm,
    key_perm,
    out_cotangent,
):
    seqs, length, width = layer_input.shape
    heads = query_perm.shape[1]
    head_size = width // heads
    scale = head_size ** (-0.5)
    tokens = seqs * length
    gathered = (
        lax.all_gather(in_weight, "shard", axis=0, tiled=True),
        lax.all_gather(query_bias, "shard", axis=0, tiled=True),
        lax.all_gather(value_bias, "shard", axis=0, tiled=True),
        lax.all_gather(out_weight, "shard", axis=0, tiled=True),
        lax.all_gather(out_bias, "shard", axis=0, tiled=True),
        lax.all_gather(first_gain, "shard", axis=0, tiled=True),
        lax.all_gather(first_shift, "shard", axis=0, tiled=True),
        lax.all_gather(inner_weight, "shard", axis=0, tiled=True),
        lax.all_gather(inner_bias, "shard", axis=0, tiled=True),
        lax.all_gather(outer_weight, "shard", axis=0, tiled=True),
        lax.all_gather(outer_bias, "shard", axis=0, tiled=True),
        lax.all_gather(second_gain, "shard", axis=0, tiled=True),
        lax.all_gather(second_shift, "shard", axis=0, tiled=True),
    )
    (
        w_in,
        b_query,
        b_value,
        w_out,
        b_out,
        g_first,
        s_first,
        w_inner,
        b_inner,
        w_outer,
        b_outer,
        g_second,
        s_second,
    ) = gathered
    flat_in = layer_input.reshape(tokens, width)
    projected = jnp.dot(flat_in, w_in, preferred_element_type=jnp.float32)
    query = (projected[:, :width] + b_query.astype(jnp.float32)).astype(jnp.bfloat16)
    keys = projected[:, width : 2 * width].astype(jnp.bfloat16)
    values = (projected[:, 2 * width :] + b_value.astype(jnp.float32)).astype(jnp.bfloat16)
    q_cl = in_clusters(arrange(to_heads(query, seqs, heads), query_perm))
    k_cl = in_clusters(arrange(to_heads(keys, seqs, heads), key_perm))
    v_cl = in_clusters(arrange(to_heads(values, seqs, heads), key_perm))
    seg_heads = jnp.broadcast_to(segment_ids[:, None, :], query_perm.shape)
    ok_heads = jnp.broadcast_to(token_valid[:, None, :], query_perm.shape)
    cshape = (seqs, heads, length // CL, CL)
    seg_query = jnp.take_along_axis(seg_heads, query_perm, axis=2).reshape(cshape)
    seg_key = jnp.take_along_axis(seg_heads, key_perm, axis=2).reshape(cshape)
    ok_query = jnp.take_along_axis(ok_heads, query_perm, axis=2).reshape(cshape)
    ok_key = jnp.take_along_axis(ok_heads, key_perm, axis=2).reshape(cshape)
    visible = (
        (seg_query[..., :, None] == seg_key[..., None, :])
        & (ok_query[..., :, None] > 0)
        & (ok_key[..., None, :] > 0)
    )
    scores = (
        jnp.einsum("shcie,shcje->shcij", q_cl, k_cl, preferred_element_type=jnp.float32) * scale
    )
    maxima = jnp.max(jnp.where(visible, scores, -1e30), axis=-1, keepdims=True)
    raised = jnp.where(visible, jnp.exp(jnp.where(visible, scores - maxima, 0.0)), 0.0)
    divisor = jnp.maximum(jnp.sum(raised, axis=-1, keepdims=True), 1.0)
    probs_low = (raised / divisor).astype(jnp.bfloat16)
    log_total = maxima + jnp.log(divisor)
    combined = jnp.einsum("shcij,shcje->shcie", probs_low, v_cl, preferred_element_type=jnp.float32)
    query_back = invert_order(query_perm)
    key_back = invert_order(key_perm)
    attended = from_heads(
        arrange(combined.reshape(seqs, heads, length, head_size), query_back)
    ).astype(jnp.bfloat16)
    branch = jnp.dot(attended, w_out, preferred_element_type=jnp.float32) + b_out.astype(
        jnp.float32
    )
    first_sum = flat_in.astype(jnp.float32) + branch
    normed_first, inv_first = norm_parts(first_sum)
    first_out = normed_first * g_first.astype(jnp.float32) + s_first.astype(jnp.float32)
    first_low = first_out.astype(jnp.bfloat16)
    inner = jnp.dot(first_low, w_inner, preferred_element_type=jnp.float32) + b_inner.astype(
        jnp.float32
    )
    activated = jax.nn.gelu(inner, approximate=False).astype(jnp.bfloat16)
    outer = jnp.dot(activated, w_outer, preferred_element_type=jnp.float32) + b_outer.astype(
        jnp.float32
    )
    normed_second, inv_second = norm_parts(first_out + outer)
    hidden_out = (
        (normed_second * g_second.astype(jnp.float32) + s_second.astype(jnp.float32))
        .astype(jnp.bfloat16)
        .reshape(seqs, length, width)
    )
    back_in, back_out, back_inner, back_outer, back_gfirst, back_gsecond = (
        w_in,
        w_out,
        w_inner,
        w_outer,
        g_first,
        g_second,
    )
    grad_top = out_cotangent.reshape(tokens, width).astype(jnp.float32)
    d_second, grad_g_second, grad_s_second = norm_back(
        grad_top, normed_second, inv_second, back_gsecond.astype(jnp.float32)
    )
    d_outer = d_second.astype(jnp.bfloat16)
    grad_b_outer = jnp.sum(d_outer, axis=0, dtype=jnp.float32)
    d_activated = jnp.einsum("td,fd->tf", d_outer, back_outer, preferred_element_type=jnp.float32)
    unused, gelu_pull = jax.vjp(partial(jax.nn.gelu, approximate=False), inner)
    d_inner = gelu_pull(d_activated)[0].astype(jnp.bfloat16)
    grad_b_inner = jnp.sum(d_inner, axis=0, dtype=jnp.float32)
    d_first_out = d_second + jnp.einsum(
        "tf,df->td", d_inner, back_inner, preferred_element_type=jnp.float32
    )
    d_first, grad_g_first, grad_s_first = norm_back(
        d_first_out, normed_first, inv_first, back_gfirst.astype(jnp.float32)
    )
    d_branch = d_first.astype(jnp.bfloat16)
    grad_b_out = jnp.sum(d_branch, axis=0, dtype=jnp.float32)
    d_attended = jnp.einsum(
        "te,de->td", d_branch, back_out, preferred_element_type=jnp.float32
    ).astype(jnp.bfloat16)
    do_cl = in_clusters(arrange(to_heads(d_attended, seqs, heads), query_perm))
    again_scores = (
        jnp.einsum("shcie,shcje->shcij", q_cl, k_cl, preferred_element_type=jnp.float32) * scale
    )
    probs = jnp.where(visible, jnp.exp(jnp.where(visible, again_scores - log_total, 0.0)), 0.0)
    d_probs = jnp.einsum("shcie,shcje->shcij", do_cl, v_cl, preferred_element_type=jnp.float32)
    row_terms = jnp.sum(probs * d_probs, axis=-1, keepdims=True)
    d_scores = (probs * (d_probs - row_terms)).astype(jnp.bfloat16)
    dq_cl = (
        jnp.einsum("shcij,shcje->shcie", d_scores, k_cl, preferred_element_type=jnp.float32) * scale
    )
    dk_cl = (
        jnp.einsum("shcij,shcie->shcje", d_scores, q_cl, preferred_element_type=jnp.float32) * scale
    )
    dv_cl = jnp.einsum(
        "shcij,shcie->shcje", probs.astype(jnp.bfloat16), do_cl, preferred_element_type=jnp.float32
    )

    def restore(clustered, back_order):
        return from_heads(arrange(clustered.reshape(seqs, heads, length, head_size), back_order))

    d_proj = jnp.concatenate(
        [restore(dq_cl, query_back), restore(dk_cl, key_back), restore(dv_cl, key_back)], axis=1
    ).astype(jnp.bfloat16)
    grad_b_query = jnp.sum(d_proj[:, :width], axis=0, dtype=jnp.float32)
    grad_b_value = jnp.sum(d_proj[:, 2 * width :], axis=0, dtype=jnp.float32)
    input_grad = (
        (d_first + jnp.einsum("te,de->td", d_proj, back_in, preferred_element_type=jnp.float32))
        .astype(jnp.bfloat16)
        .reshape(seqs, length, width)
    )
    local_shapes = [
        in_weight.shape,
        query_bias.shape,
        value_bias.shape,
        out_weight.shape,
        out_bias.shape,
        first_gain.shape,
        first_shift.shape,
        inner_weight.shape,
        inner_bias.shape,
        outer_weight.shape,
        outer_bias.shape,
        second_gain.shape,
        second_shift.shape,
    ]

    def product_rows(left, right):
        return jnp.einsum("tk,te->ke", left, right, preferred_element_type=jnp.float32).reshape(
            lax.axis_size("shard") * 1, -1
        )

    def vector_rows(vector):
        return vector.reshape(lax.axis_size("shard") * 1, -1)

    pieces = [
        product_rows(flat_in, d_proj),
        vector_rows(grad_b_query),
        vector_rows(grad_b_value),
        product_rows(attended, d_branch),
        vector_rows(grad_b_out),
        vector_rows(grad_g_first),
        vector_rows(grad_s_first),
        product_rows(first_low, d_inner),
        vector_rows(grad_b_inner),
        product_rows(activated, d_outer),
        vector_rows(grad_b_outer),
        vector_rows(grad_g_second),
        vector_rows(grad_s_second),
    ]
    my_rows = lax.psum_scatter(
        jnp.concatenate(pieces, axis=1), "shard", scatter_dimension=0, tiled=True
    )
    my_rows = lax.psum(my_rows.astype(jnp.bfloat16), "rep").astype(jnp.float32)
    flat_mine = my_rows.reshape(-1)
    results = []
    offset = 0
    for shape_here in local_shapes:
        count_here = 1
        for extent_here in shape_here:
            count_here = count_here * extent_here
        results.append(flat_mine[offset : offset + count_here].reshape(shape_here))
        offset = offset + count_here
    return (
        hidden_out,
        input_grad,
        results[0],
        results[1],
        results[2],
        results[3],
        results[4],
        results[5],
        results[6],
        results[7],
        results[8],
        results[9],
        results[10],
        results[11],
        results[12],
    )


def solution(mesh):
    return jax.shard_map(
        shards,
        mesh=mesh,
        in_specs=(
            P(("rep", "shard"), None, None),
            P("shard", None),
            P("shard"),
            P("shard"),
            P("shard", None),
            P("shard"),
            P("shard"),
            P("shard"),
            P("shard", None),
            P("shard"),
            P("shard", None),
            P("shard"),
            P("shard"),
            P("shard"),
            P(("rep", "shard"), None),
            P(("rep", "shard"), None),
            P(("rep", "shard"), None, None),
            P(("rep", "shard"), None, None),
            P(("rep", "shard"), None, None),
        ),
        out_specs=(
            P(("rep", "shard"), None, None),
            P(("rep", "shard"), None, None),
            P("shard", None),
            P("shard"),
            P("shard"),
            P("shard", None),
            P("shard"),
            P("shard"),
            P("shard"),
            P("shard", None),
            P("shard"),
            P("shard", None),
            P("shard"),
            P("shard"),
            P("shard"),
        ),
        check_vma=False,
    )
```

profile of v0, /device:TPU:0, one launch (start us, length us, event | category | flops | bytes accessed | tf_op | source)
XLA Modules:
  0.0 3090.1 jit_solution(8853044434371541928)
XLA Ops:
  13.8 97.2 %gather_fusion.2 = s32[12288]{0:T(1024)S(1)} fusion(s32[12,1024]{1,0:T(8,128)S(1)} %broadcast.664, s32[12288]{0:T(1024)S(1)} %bitcast.233), kind=kCustom, calls=%fused_computation.4.clone | custom fusion | bytes 196608 | tf_op jit(solution)/shard_map/jit(take_along_axis)/gather | solution.py:127
  111.1 97.2 %gather_fusion = s32[12288]{0:T(1024)S(1)} fusion(s32[12,1024]{1,0:T(8,128)S(1)} %broadcast.662, s32[12288]{0:T(1024)S(1)} %bitcast.234), kind=kCustom, calls=%fused_computation.clone | custom fusion | bytes 196608 | tf_op jit(solution)/shard_map/jit(take_along_axis)/gather | solution.py:125
  208.4 97.2 %gather_fusion.3 = s32[12288]{0:T(1024)S(1)} fusion(s32[12,1024]{1,0:T(8,128)S(1)} %broadcast.664, s32[12288]{0:T(1024)S(1)} %bitcast.235), kind=kCustom, calls=%fused_computation.5.clone | custom fusion | bytes 196608 | tf_op jit(solution)/shard_map/jit(take_along_axis)/gather | solution.py:128
  305.8 97.2 %gather_fusion.1 = s32[12288]{0:T(1024)S(1)} fusion(s32[12,1024]{1,0:T(8,128)S(1)} %broadcast.662, s32[12288]{0:T(1024)S(1)} %bitcast.236), kind=kCustom, calls=%fused_computation.3.clone | custom fusion | bytes 196608 | tf_op jit(solution)/shard_map/jit(take_along_axis)/gather | solution.py:126
  404.7 45.4 %scatter_custom_fusion.1 = s32[12288]{0:T(1024)S(1)} fusion(s32[12288]{0:T(1024)S(1)} %reshape.572, s32[12288]{0:T(1024)S(1)} %reshape.566, s32[]{:T(128)} %constant.12.clone.1), kind=kCustom, calls=%fused_computation.151 | custom fusion | bytes 49156
  450.9 45.4 %scatter_custom_fusion = s32[12288]{0:T(1024)S(1)} fusion(s32[12288]{0:T(1024)S(1)} %reshape.564, s32[12288]{0:T(1024)S(1)} %reshape.566, s32[]{:T(128)} %constant.12.clone.1), kind=kCustom, calls=%fused_computation.153 | custom fusion | bytes 49156
  499.6 38.8 %all-reduce.9 = (bf16[768]{0:T(1024)(128)(2,1)S(1)}, bf16[768]{0:T(1024)(128)(2,1)S(1)}, bf16[768]{0:T(1024)(128)(2,1)S(1)}, bf16[768]{0:T(1024)(128)(2,1)S(1)},...) all-reduce(bf16[768]{0:T(1024)(128)(2,1)S(1)} %dynamic-update-slice, ...), channel_id=1, replica_groups=mesh['rep'=4,'shard'=8] {'shard'}, use_global_device_ids=true, to_apply=%add | all-reduce | flops 6144 | bytes 24576
  540.2 25.9 all-gather
  572.3 5.8 fusion.27
  586.3 119.4 %gather_fusion.5 = bf16[12288,64]{1,0:T(8,128)(2,1)} fusion(bf16[12,1024,64]{2,1,0:T(8,128)(2,1)S(1)} %bitcast.237, s32[12288]{0:T(1024)S(1)} %bitcast.231), kind=kCustom, calls=%fused_computation.6.clone | custom fusion | bytes 3244032 | tf_op jit(solution)/shard_map/jit(take_along_axis)/gather | solution.py:50
  705.7 4.3 copy.98
  713.0 119.4 %gather_fusion.6 = bf16[12288,64]{1,0:T(8,128)(2,1)} fusion(bf16[12,1024,64]{2,1,0:T(8,128)(2,1)S(1)} %bitcast.238, s32[12288]{0:T(1024)S(1)} %bitcast.232), kind=kCustom, calls=%fused_computation.7.clone | custom fusion | bytes 3244032 | tf_op jit(solution)/shard_map/jit(take_along_axis)/gather | solution.py:50
  844.0 119.4 %gather_fusion.4 = bf16[12288,64]{1,0:T(8,128)(2,1)} fusion(bf16[12,1024,64]{2,1,0:T(8,128)(2,1)S(1)} %bitcast.239, s32[12288]{0:T(1024)S(1)} %bitcast.229), kind=kCustom, calls=%fused_computation.1.clone | custom fusion | bytes 3244032 | tf_op jit(solution)/shard_map/jit(take_along_axis)/gather | solution.py:50
  967.2 12.3 select_reduce_fusion
  979.6 4.9 fusion.11
  985.1 8.2 fusion.20
  993.4 119.5 %gather_fusion.7 = bf16[12288,64]{1,0:T(8,128)(2,1)} fusion(bf16[12,1024,64]{2,1,0:T(8,128)(2,1)S(1)} %bitcast.244, s32[12288]{0:T(1024)S(1)} %reshape.741), kind=kCustom, calls=%fused_computation.2.clone | custom fusion | bytes 3244032 | tf_op jit(solution)/shard_map/jit(take_along_axis)/gather | solution.py:50
  1122.0 38.7 %multiply_convert_fusion = (bf16[1024,3072]{1,0:T(8,128)(2,1)}, f32[1024,3072]{1,0:T(8,128)}, f32[1024,3072]{1,0:T(8,128)}) fusion(f32[3072]{0:T(1024)S(1)} %bitcast.302, bf16[768,3072]{1,0:T(8,128)(2,1)} %all-gather.10.cloned.1.call-done, f32[1024,768]{0,1:T(8,128)S(1)} %get-tuple-element.122, f32[768]{0:T(1024)S(1)} %convert_element_type.123, ...), kind=kOutput, calls=%fused_computation.18 | convolution fusion | flops 5043388416 | bytes 39348224 | tf_op jit(solution)/shard_map/dot_general | solution.py:155
  1160.7 9.8 fusion.64
  1174.9 7.5 fusion.65
  1182.4 17.4 convert_reduce_fusion
  1199.9 10.6 fusion.56
  1210.5 9.0 multiply_reduce_fusion.1
  1229.4 119.4 %gather_fusion.8 = bf16[12288,64]{1,0:T(8,128)(2,1)} fusion(bf16[12,1024,64]{2,1,0:T(8,128)(2,1)S(1)} %bitcast.240, s32[12288]{0:T(1024)S(1)} %bitcast.230), kind=kCustom, calls=%fused_computation.8.clone | custom fusion | bytes 3244032 | tf_op jit(solution)/shard_map/jit(take_along_axis)/gather | solution.py:50
  1352.7 8.2 fusion.18
  1360.9 12.2 multiply_reduce_fusion
  1373.1 5.0 multiply_convert_fusion.1
  1384.1 9.0 reshape.425
  1399.2 120.2 %gather_fusion.11 = bf16[12288,64]{1,0:T(8,128)(2,1)} fusion(bf16[12,1024,64]{2,1,0:T(8,128)(2,1)S(1)} %bitcast.243, s32[12288]{0:T(1024)S(1)} %copy-done.4), kind=kCustom, calls=%fused_computation.11.clone | custom fusion | bytes 3244032 | tf_op jit(solution)/shard_map/jit(take_along_axis)/gather | solution.py:50
  1519.4 4.5 copy.130
  1523.9 9.0 reshape.427
  1536.0 120.3 %gather_fusion.9 = bf16[12288,64]{1,0:T(8,128)(2,1)} fusion(bf16[12,1024,64]{2,1,0:T(8,128)(2,1)S(1)} %bitcast.241, s32[12288]{0:T(1024)S(1)} %copy-done.6), kind=kCustom, calls=%fused_computation.9.clone | custom fusion | bytes 3244032 | tf_op jit(solution)/shard_map/jit(take_along_axis)/gather | solution.py:50
  1664.5 120.3 %gather_fusion.10 = bf16[12288,64]{1,0:T(8,128)(2,1)} fusion(bf16[12,1024,64]{2,1,0:T(8,128)(2,1)S(1)} %bitcast.242, s32[12288]{0:T(1024)S(1)} %copy-done.4), kind=kCustom, calls=%fused_computation.10.clone | custom fusion | bytes 3244032 | tf_op jit(solution)/shard_map/jit(take_along_axis)/gather | solution.py:50
  1784.8 4.3 copy.125
  1793.7 8.9 convolution_bitcast_fusion
  1802.6 8.0 copy.132
  1810.6 7.2 reshape.418
  1817.8 5.3 constant_dynamic-update-slice_fusion
  1826.2 7.5 dynamic-update-slice.11
  1837.9 26.4 dynamic-update-slice.15
  1865.8 26.0 dynamic-update-slice.17
  1896.0 1069.1 %all-reduce.14 = bf16[8,885888]{1,0:T(8,128)(2,1)} all-reduce(f32[8,885888]{1,0:T(8,128)} %dynamic-update-slice.20), channel_id=2, replica_groups=mesh['rep'=4,'shard'=8] {'shard'}, use_global_device_ids=true, to_apply=%region_22.26.clone | all-reduce | flops 7087104 | bytes 42522624
  2965.1 9.1 dynamic-slice_convert_fusion
  2974.2 8.5 fusion.29
  2985.3 63.7 %all-reduce.13.cloned.1.call-done = bf16[1,885888]{1,0:T(2,128)(2,1)} async-done(((bf16[1,885888]{1,0:T(2,128)(2,1)}), bf16[1,885888]{1,0:T(2,128)(2,1)}) %all-reduce.13.cloned.1.call-update) | async-done | bytes 1771792 | tf_op jit(solution)/shard_map/psum | solution.py:270
  3049.0 6.3 convert_element_type.146
  3057.3 9.1 slice_reduce_fusion.2
  3066.5 12.7 slice_reduce_fusion
  (292 shorter events, 123.3 us)
Async XLA Ops:
  7.2 6.6 copy-start
  7.2 565.1 %all-gather.6.cloned.1.call-start = ((), (), s32[]{:S(2)}) async-start(), calls=%async_computation | async-start | bytes 3981312 | tf_op jit(solution)/shard_map/all_gather | solution.py:85
  7.9 1109.7 %all-gather.8.cloned.1.call-start = ((), (), s32[]{:S(2)}) async-start(), calls=%async_computation.1 | async-start | bytes 1327104 | tf_op jit(solution)/shard_map/all_gather | solution.py:88
  8.7 1113.3 %all-gather.10.cloned.1.call-start = ((), (), s32[]{:S(2)}) async-start(), calls=%async_computation.2 | async-start | bytes 5308416 | tf_op jit(solution)/shard_map/all_gather | solution.py:92
  9.4 1151.3 %all-gather.12.cloned.1.call-start = ((), (), s32[]{:S(2)}) async-start(), calls=%async_computation.3 | async-start | bytes 5308416 | tf_op jit(solution)/shard_map/all_gather | solution.py:94
  10.0 3039.0 %all-reduce.13.cloned.1.call-start = ((), (), s32[]{:S(2)}) async-start(), calls=%async_computation.4 | async-start | bytes 7087104 | tf_op jit(solution)/shard_map/psum | solution.py:270
  11.9 832.0 %copy-start.2 = (s32[12,1024,1]{1,2,0:T(1,128)}, s32[12,1024,1]{1,2,0:T(1,128)S(1)}, u32[]{:S(2)}) copy-start(s32[12,1024,1]{1,2,0:T(1,128)S(1)} %get-tuple-element.110) | copy-start | bytes 147460
  13.8 97.3 %copy-start.49 = (s32[1,1024]{1,0:T(1,128)S(1)}, s32[1,1024]{1,0:T(1,128)}, u32[]{:S(2)}) copy-start(s32[1,1024]{1,0:T(1,128)} %param.39) | copy-start | bytes 12292
  305.6 97.5 %copy-start.30 = (s32[1,12,1024]{2,0,1:T(1,128)S(1)}, s32[1,12,1024]{2,0,1:T(1,128)}, u32[]{:S(2)}) copy-start(s32[1,12,1024]{2,0,1:T(1,128)} %param.41) | copy-start | bytes 147460
  305.6 97.6 %copy-start.31 = (s32[1,12,1024]{2,0,1:T(1,128)S(1)}, s32[1,12,1024]{2,0,1:T(1,128)}, u32[]{:S(2)}) copy-start(s32[1,12,1024]{2,0,1:T(1,128)} %param.42) | copy-start | bytes 147460
  305.6 97.8 %copy-start.54 = (s32[3]{0:T(128)S(1)}, s32[3]{0:T(128)}, u32[]{:S(2)}) copy-start(s32[3]{0:T(128)} %constant.125) | copy-start | bytes 40
  305.6 98.4 %copy-start.53 = (s32[3]{0:T(128)S(1)}, s32[3]{0:T(128)}, u32[]{:S(2)}) copy-start(s32[3]{0:T(128)} %constant.128) | copy-start | bytes 40
  305.6 190.7 %copy-start.52 = (bf16[384]{0:T(512)(128)(2,1)S(1)}, bf16[384]{0:T(512)(128)(2,1)}, u32[]{:S(2)}) copy-start(bf16[384]{0:T(512)(128)(2,1)} %param.34) | copy-start | bytes 2308
  305.7 190.8 %copy-start.51 = (u32[32]{0:T(128)S(1)}, u32[32]{0:T(128)}, u32[]{:S(2)}) copy-start(u32[32]{0:T(128)} %constant.300) | copy-start | bytes 388
  305.7 192.0 %copy-start.56 = (bf16[96]{0:T(256)(128)(2,1)S(1)}, bf16[96]{0:T(256)(128)(2,1)}, u32[]{:S(2)}) copy-start(bf16[96]{0:T(256)(128)(2,1)} %param.38) | copy-start | bytes 580
  305.7 192.2 %copy-start.57 = (bf16[96]{0:T(256)(128)(2,1)S(1)}, bf16[96]{0:T(256)(128)(2,1)}, u32[]{:S(2)}) copy-start(bf16[96]{0:T(256)(128)(2,1)} %param.36) | copy-start | bytes 580
  305.7 192.5 %copy-start.58 = (bf16[96]{0:T(256)(128)(2,1)S(1)}, bf16[96]{0:T(256)(128)(2,1)}, u32[]{:S(2)}) copy-start(bf16[96]{0:T(256)(128)(2,1)} %param.31) | copy-start | bytes 580
  305.7 192.7 %copy-start.59 = (bf16[96]{0:T(256)(128)(2,1)S(1)}, bf16[96]{0:T(256)(128)(2,1)}, u32[]{:S(2)}) copy-start(bf16[96]{0:T(256)(128)(2,1)} %param.32) | copy-start | bytes 580
  305.7 192.9 %copy-start.60 = (bf16[96]{0:T(256)(128)(2,1)S(1)}, bf16[96]{0:T(256)(128)(2,1)}, u32[]{:S(2)}) copy-start(bf16[96]{0:T(256)(128)(2,1)} %param.30) | copy-start | bytes 580
  305.7 193.1 %copy-start.61 = (bf16[96]{0:T(256)(128)(2,1)S(1)}, bf16[96]{0:T(256)(128)(2,1)}, u32[]{:S(2)}) copy-start(bf16[96]{0:T(256)(128)(2,1)} %param.28) | copy-start | bytes 580
  305.7 193.4 %copy-start.62 = (bf16[96]{0:T(256)(128)(2,1)S(1)}, bf16[96]{0:T(256)(128)(2,1)}, u32[]{:S(2)}) copy-start(bf16[96]{0:T(256)(128)(2,1)} %param.27) | copy-start | bytes 580
  305.8 193.6 %copy-start.63 = (bf16[96]{0:T(256)(128)(2,1)S(1)}, bf16[96]{0:T(256)(128)(2,1)}, u32[]{:S(2)}) copy-start(bf16[96]{0:T(256)(128)(2,1)} %param.37) | copy-start | bytes 580
  403.0 164.4 %copy-start.25 = (bf16[1,1024,768]{2,1,0:T(8,128)(2,1)S(1)}, bf16[1,1024,768]{2,1,0:T(8,128)(2,1)}, u32[]{:S(2)}) copy-start(bf16[1,1024,768]{2,1,0:T(8,128)(2,1)} %param.43) | copy-start | bytes 4718596
  403.2 581.9 %copy-start.32 = (s32[1,12,1024]{2,0,1:T(1,128)}, s32[1,12,1024]{2,0,1:T(1,128)S(1)}, u32[]{:S(2)}) copy-start(s32[1,12,1024]{2,0,1:T(1,128)S(1)} %get-tuple-element.108) | copy-start | bytes 147460
  403.4 581.7 %copy-start.34 = (s32[1,12,1024]{2,0,1:T(1,128)}, s32[1,12,1024]{2,0,1:T(1,128)S(1)}, u32[]{:S(2)}) copy-start(s32[1,12,1024]{2,0,1:T(1,128)S(1)} %get-tuple-element.106) | copy-start | bytes 147460
  496.3 619.7 %copy-start.37 = (pred[12,1024]{1,0:T(8,128)(4,1)}, pred[12,1024]{1,0:T(8,128)(4,1)S(1)}, u32[]{:S(2)}) copy-start(pred[12,1024]{1,0:T(8,128)(4,1)S(1)} %and_bitcast_fusion.1) | copy-start | bytes 36868
  566.1 400.4 %copy-start.39 = (pred[1,12,1024,1]{2,1,3,0:T(8,128)(4,1)}, pred[1,12,1024,1]{2,1,3,0:T(8,128)(4,1)S(1)}, u32[]{:S(2)}) copy-start(pred[1,12,1024,1]{2,1,3,0:T(8,128)(4,1)S(1)} %copy.184) | copy-start | bytes 36868
  566.4 418.6 %copy-start.41 = (pred[12,8,128]{2,1,0:T(8,128)(4,1)}, pred[12,8,128]{2,1,0:T(8,128)(4,1)S(1)}, u32[]{:S(2)}) copy-start(pred[12,8,128]{2,1,0:T(8,128)(4,1)S(1)} %slice.147) | copy-start | bytes 36868
  566.7 418.4 %copy-start.43 = (pred[12,8,128]{2,1,0:T(8,128)(4,1)}, pred[12,8,128]{2,1,0:T(8,128)(4,1)S(1)}, u32[]{:S(2)}) copy-start(pred[12,8,128]{2,1,0:T(8,128)(4,1)S(1)} %slice.148) | copy-start | bytes 36868
  567.4 426.0 %copy-start.5 = (s32[12288]{0:T(1024)}, s32[12288]{0:T(1024)S(1)}, u32[]{:S(2)}) copy-start(s32[12288]{0:T(1024)S(1)} %reshape.741) | copy-start | bytes 147460
  568.6 9.5 copy-start.8
  967.2 12.3 copy-start.18
  979.5 13.8 copy-start.7
  1121.5 39.1 %copy-start.10 = (f32[1024,768]{0,1:T(8,128)}, f32[1024,768]{0,1:T(8,128)S(1)}, u32[]{:S(2)}) copy-start(f32[1024,768]{0,1:T(8,128)S(1)} %get-tuple-element.122) | copy-start | bytes 9437188
  1122.0 38.7 %copy-start.50 = (f32[768]{0:T(1024)S(1)}, f32[768]{0:T(1024)}, u32[]{:S(2)}) copy-start(f32[768]{0:T(1024)} %convert_element_type.127) | copy-start | bytes 9220
  1160.7 10.2 copy-start.9
  1160.7 10.2 copy-start.46
  1199.8 10.6 copy-start.11
  1199.8 10.6 copy-start.64
  1352.0 8.9 slice-start
  1352.7 8.2 slice-start.1
  1352.7 8.2 copy-start.28
  1793.3 9.3 copy-start.20
  1817.8 8.4 copy-start.12
  1865.7 28.9 copy-start.48
  2965.1 9.1 copy-start.15
  2965.1 9.2 copy-start.21
  3066.5 17.0 copy-start.1
  (26 other events, 92.0 us)
Sparse Core Ops, SparseCore 0:
  10.2 67.8 all-gather.5
  80.3 39.5 all-gather.7
  122.1 78.6 all-gather.9
  202.8 78.0 all-gather.11
  2974.3 74.5 all-reduce.12
where the time goes:
time: 3100 us; the launch traced here: 3090 us
  local copies, waits for them, and re-layouts  1660 us (54%)
  blocking collectives  1130 us (36%)
  matrix products  172 us (6%)
  waiting for transfers between devices  66.3 us (2%)
  other arithmetic  40.3 us (1%)
    unnamed x2, blocking collectives  1110 us
    gather x18, local copies, waits for them, and re-layouts, arrange(): return jnp.take_along_axis(tensor, order[..., None], axis=2)  987 us
    unnamed x186, local copies, waits for them, and re-layouts  185 us
    gather x1, local copies, waits for them, and re-layouts, shards(): ok_query = jnp.take_along_axis(ok_heads, query_perm, axis=2).reshape(cshape)  97.2 us
    gather x1, local copies, waits for them, and re-layouts, shards(): jnp.take_along_axis(seg_heads, query_perm, axis=2).reshape(cshape)  97.2 us
    gather x1, local copies, waits for them, and re-layouts, shards(): ok_key = jnp.take_along_axis(ok_heads, key_perm, axis=2).reshape(cshape)  97.2 us
    gather x1, local copies, waits for them, and re-layouts, shards(): seg_key = jnp.take_along_axis(seg_heads, key_perm, axis=2).reshape(cshape)  97.2 us
    psum x1, waiting for transfers between devices, shards(): my_rows = lax.psum(my_rows.astype(jnp.bfloat16), 'rep').astype(jnp.float32)  63.7 us
  transfers between devices with their start and end apart: 5, of which 1 were waited for; matrix products, arithmetic and copies ran while one was open for 35% of the time, Pallas kernels for 0%

commit v1 on v0

--- a/solution.py
+++ b/solution.py
@@ -267,7 +267,9 @@
     my_rows = lax.psum_scatter(
         jnp.concatenate(pieces, axis=1), "shard", scatter_dimension=0, tiled=True
     )
-    my_rows = lax.psum(my_rows.astype(jnp.bfloat16), "rep").astype(jnp.float32)
+    my_rows = jnp.sum(lax.all_gather(my_rows.astype(jnp.bfloat16), "rep"), axis=0).astype(
+        jnp.float32
+    )
     flat_mine = my_rows.reshape(-1)
     results = []
     offset = 0

time: 3100 us -> 3170 us (1.023)
  other arithmetic: 40.3 us -> 72.3 us
    all_gather x0 -> x1, waiting for transfers between devices: none -> 79.8 us  [shards(): lax.all_gather(my_rows.astype(jnp.bfloat16), 'rep')]
    psum x1 -> x0, waiting for transfers between devices: 63.7 us -> none  [shards(): my_rows = lax.psum(my_rows.astype(jnp.bfloat16), 'rep').astype(jnp.float32)]
    reduce_sum x0 -> x1, other arithmetic: none -> 38.3 us  [shards(): jnp.sum(lax.all_gather(my_rows.astype(jnp.bfloat16), 'rep'), axis=0)]
    unnamed x186 -> x187, local copies, waits for them, and re-layouts: 185 us -> 192 us
where the time goes in v1:
time: 3170 us; the launch traced here: 3160 us
  local copies, waits for them, and re-layouts  1680 us (53%)
  blocking collectives  1130 us (36%)
  matrix products  171 us (5%)
  waiting for transfers between devices  82.4 us (3%)
  other arithmetic  72.3 us (2%)
    unnamed x2, blocking collectives  1110 us
    gather x18, local copies, waits for them, and re-layouts, arrange(): return jnp.take_along_axis(tensor, order[..., None], axis=2)  987 us
    unnamed x187, local copies, waits for them, and re-layouts  192 us
    gather x1, local copies, waits for them, and re-layouts, shards(): ok_key = jnp.take_along_axis(ok_heads, key_perm, axis=2).reshape(cshape)  97.2 us
    gather x1, local copies, waits for them, and re-layouts, shards(): seg_key = jnp.take_along_axis(seg_heads, key_perm, axis=2).reshape(cshape)  97.2 us
    gather x1, local copies, waits for them, and re-layouts, shards(): ok_query = jnp.take_along_axis(ok_heads, query_perm, axis=2).reshape(cshape)  97.2 us
    gather x1, local copies, waits for them, and re-layouts, shards(): jnp.take_along_axis(seg_heads, query_perm, axis=2).reshape(cshape)  97.2 us
    all_gather x1, waiting for transfers between devices, shards(): lax.all_gather(my_rows.astype(jnp.bfloat16), 'rep')  79.8 us
  transfers between devices with their start and end apart: 5, of which 1 were waited for; matrix products, arithmetic and copies ran while one was open for 35% of the time, Pallas kernels for 0%

profile of v1, /device:TPU:0, one launch (start us, length us, event | category | flops | bytes accessed | tf_op | source)
XLA Modules:
  0.0 3157.3 jit_solution(6086148110228714409)
XLA Ops:
  13.8 97.2 %gather_fusion.2 = s32[12288]{0:T(1024)S(1)} fusion(s32[12,1024]{1,0:T(8,128)S(1)} %broadcast.664, s32[12288]{0:T(1024)S(1)} %bitcast.235), kind=kCustom, calls=%fused_computation.4.clone | custom fusion | bytes 196608 | tf_op jit(solution)/shard_map/jit(take_along_axis)/gather | solution.py:127
  111.1 97.2 %gather_fusion = s32[12288]{0:T(1024)S(1)} fusion(s32[12,1024]{1,0:T(8,128)S(1)} %broadcast.662, s32[12288]{0:T(1024)S(1)} %bitcast.236), kind=kCustom, calls=%fused_computation.clone | custom fusion | bytes 196608 | tf_op jit(solution)/shard_map/jit(take_along_axis)/gather | solution.py:125
  208.4 97.2 %gather_fusion.3 = s32[12288]{0:T(1024)S(1)} fusion(s32[12,1024]{1,0:T(8,128)S(1)} %broadcast.664, s32[12288]{0:T(1024)S(1)} %bitcast.237), kind=kCustom, calls=%fused_computation.5.clone | custom fusion | bytes 196608 | tf_op jit(solution)/shard_map/jit(take_along_axis)/gather | solution.py:128
  305.8 97.2 %gather_fusion.1 = s32[12288]{0:T(1024)S(1)} fusion(s32[12,1024]{1,0:T(8,128)S(1)} %broadcast.662, s32[12288]{0:T(1024)S(1)} %bitcast.238), kind=kCustom, calls=%fused_computation.3.clone | custom fusion | bytes 196608 | tf_op jit(solution)/shard_map/jit(take_along_axis)/gather | solution.py:126
  404.7 45.4 %scatter_custom_fusion.1 = s32[12288]{0:T(1024)S(1)} fusion(s32[12288]{0:T(1024)S(1)} %reshape.584, s32[12288]{0:T(1024)S(1)} %reshape.578, s32[]{:T(128)} %constant.17.clone.1), kind=kCustom, calls=%fused_computation.152 | custom fusion | bytes 49156
  450.9 45.4 %scatter_custom_fusion = s32[12288]{0:T(1024)S(1)} fusion(s32[12288]{0:T(1024)S(1)} %reshape.576, s32[12288]{0:T(1024)S(1)} %reshape.578, s32[]{:T(128)} %constant.17.clone.1), kind=kCustom, calls=%fused_computation.154 | custom fusion | bytes 49156
  499.6 38.8 %all-reduce.9 = (bf16[768]{0:T(1024)(128)(2,1)S(1)}, bf16[768]{0:T(1024)(128)(2,1)S(1)}, bf16[768]{0:T(1024)(128)(2,1)S(1)}, bf16[768]{0:T(1024)(128)(2,1)S(1)},...) all-reduce(bf16[768]{0:T(1024)(128)(2,1)S(1)} %dynamic-update-slice, ...), channel_id=1, replica_groups=mesh['rep'=4,'shard'=8] {'shard'}, use_global_device_ids=true, to_apply=%add | all-reduce | flops 6144 | bytes 24576
  540.2 25.9 all-gather.1
  572.3 5.8 fusion.28
  586.3 119.4 %gather_fusion.5 = bf16[12288,64]{1,0:T(8,128)(2,1)} fusion(bf16[12,1024,64]{2,1,0:T(8,128)(2,1)S(1)} %bitcast.239, s32[12288]{0:T(1024)S(1)} %bitcast.233), kind=kCustom, calls=%fused_computation.6.clone | custom fusion | bytes 3244032 | tf_op jit(solution)/shard_map/jit(take_along_axis)/gather | solution.py:50
  713.0 119.4 %gather_fusion.6 = bf16[12288,64]{1,0:T(8,128)(2,1)} fusion(bf16[12,1024,64]{2,1,0:T(8,128)(2,1)S(1)} %bitcast.240, s32[12288]{0:T(1024)S(1)} %bitcast.234), kind=kCustom, calls=%fused_computation.7.clone | custom fusion | bytes 3244032 | tf_op jit(solution)/shard_map/jit(take_along_axis)/gather | solution.py:50
  844.0 119.4 %gather_fusion.4 = bf16[12288,64]{1,0:T(8,128)(2,1)} fusion(bf16[12,1024,64]{2,1,0:T(8,128)(2,1)S(1)} %bitcast.241, s32[12288]{0:T(1024)S(1)} %bitcast.231), kind=kCustom, calls=%fused_computation.1.clone | custom fusion | bytes 3244032 | tf_op jit(solution)/shard_map/jit(take_along_axis)/gather | solution.py:50
  967.2 12.3 select_reduce_fusion
  979.6 4.9 fusion.12
  985.1 8.2 fusion.21
  993.4 119.5 %gather_fusion.7 = bf16[12288,64]{1,0:T(8,128)(2,1)} fusion(bf16[12,1024,64]{2,1,0:T(8,128)(2,1)S(1)} %bitcast.246, s32[12288]{0:T(1024)S(1)} %reshape.757), kind=kCustom, calls=%fused_computation.2.clone | custom fusion | bytes 3244032 | tf_op jit(solution)/shard_map/jit(take_along_axis)/gather | solution.py:50
  1122.0 38.7 %multiply_convert_fusion = (bf16[1024,3072]{1,0:T(8,128)(2,1)}, f32[1024,3072]{1,0:T(8,128)}, f32[1024,3072]{1,0:T(8,128)}) fusion(f32[3072]{0:T(1024)S(1)} %bitcast.304, bf16[768,3072]{1,0:T(8,128)(2,1)} %all-gather.13.cloned.1.call-done, f32[1024,768]{0,1:T(8,128)S(1)} %get-tuple-element.122, f32[768]{0:T(1024)S(1)} %convert_element_type.136, ...), kind=kOutput, calls=%fused_computation.18 | convolution fusion | flops 5043388416 | bytes 39348224 | tf_op jit(solution)/shard_map/dot_general | solution.py:155
  1160.7 9.8 fusion.65
  1174.9 7.5 fusion.66
  1182.4 17.4 convert_reduce_fusion
  1199.9 10.6 fusion.57
  1210.5 9.0 multiply_reduce_fusion.1
  1229.4 119.4 %gather_fusion.8 = bf16[12288,64]{1,0:T(8,128)(2,1)} fusion(bf16[12,1024,64]{2,1,0:T(8,128)(2,1)S(1)} %bitcast.242, s32[12288]{0:T(1024)S(1)} %bitcast.232), kind=kCustom, calls=%fused_computation.8.clone | custom fusion | bytes 3244032 | tf_op jit(solution)/shard_map/jit(take_along_axis)/gather | solution.py:50
  1352.7 8.2 fusion.19
  1360.9 12.2 multiply_reduce_fusion
  1373.1 5.0 multiply_convert_fusion.1
  1384.1 9.0 reshape.436
  1396.7 120.2 %gather_fusion.11 = bf16[12288,64]{1,0:T(8,128)(2,1)} fusion(bf16[12,1024,64]{2,1,0:T(8,128)(2,1)S(1)} %bitcast.245, s32[12288]{0:T(1024)S(1)} %copy-done.4), kind=kCustom, calls=%fused_computation.11.clone | custom fusion | bytes 3244032 | tf_op jit(solution)/shard_map/jit(take_along_axis)/gather | solution.py:50
  1516.9 4.5 copy.130
  1521.4 9.0 reshape.438
  1533.4 120.3 %gather_fusion.9 = bf16[12288,64]{1,0:T(8,128)(2,1)} fusion(bf16[12,1024,64]{2,1,0:T(8,128)(2,1)S(1)} %bitcast.243, s32[12288]{0:T(1024)S(1)} %copy-done.6), kind=kCustom, calls=%fused_computation.9.clone | custom fusion | bytes 3244032 | tf_op jit(solution)/shard_map/jit(take_along_axis)/gather | solution.py:50
  1662.0 120.3 %gather_fusion.10 = bf16[12288,64]{1,0:T(8,128)(2,1)} fusion(bf16[12,1024,64]{2,1,0:T(8,128)(2,1)S(1)} %bitcast.244, s32[12288]{0:T(1024)S(1)} %copy-done.4), kind=kCustom, calls=%fused_computation.10.clone | custom fusion | bytes 3244032 | tf_op jit(solution)/shard_map/jit(take_along_axis)/gather | solution.py:50
  1782.3 4.3 copy.125
  1791.2 8.9 convolution_bitcast_fusion
  1800.1 8.0 copy.132
  1808.1 7.2 reshape.429
  1815.3 5.3 constant_dynamic-update-slice_fusion
  1823.7 7.5 dynamic-update-slice.11
  1835.4 26.4 dynamic-update-slice.15
  1863.2 26.0 dynamic-update-slice.17
  1893.5 1069.1 %all-reduce.11 = bf16[8,885888]{1,0:T(8,128)(2,1)} all-reduce(f32[8,885888]{1,0:T(8,128)} %dynamic-update-slice.20), channel_id=3, replica_groups=mesh['rep'=4,'shard'=8] {'shard'}, use_global_device_ids=true, to_apply=%region_22.26.clone | all-reduce | flops 7087104 | bytes 42522624
  2962.6 8.9 fusion.11
  2973.1 7.8 fusion.30
  2982.5 79.8 %all-gather.17.cloned.1.call-done = bf16[4,1,885888]{2,1,0:T(2,128)(2,1)} async-done(((bf16[1,1,885888]{2,1,0:T(2,128)(2,1)}), bf16[4,1,885888]{2,1,0:T(2,128)(2,1)}) %all-gather.17.cloned.1.call-update) | async-done | bytes 7087120 | tf_op jit(solution)/shard_map/all_gather | solution.py:270
  3062.2 38.3 %reduce.17 = bf16[885888]{0:T(1024)(128)(2,1)S(1)} reduce(bf16[4,1,885888]{2,1,0:T(2,128)(2,1)} %all-gather.17.cloned.1.call-done, bf16[]{:T(256)} %constant.59.clone.1), dimensions={0,1}, to_apply=%region_23.27 | reduce | flops 2657664 | bytes 8858882 | tf_op jit(solution)/shard_map/reduce_sum | solution.py:270
  3100.6 20.2 reshape.473
  3123.5 9.3 slice_reduce_fusion.2
  3132.8 12.5 slice_reduce_fusion
  (293 shorter events, 127.3 us)
Async XLA Ops:
  7.2 6.6 copy-start
  7.2 565.1 %all-gather.9.cloned.1.call-start = ((), (), s32[]{:S(2)}) async-start(), calls=%async_computation | async-start | bytes 3981312 | tf_op jit(solution)/shard_map/all_gather | solution.py:85
  7.9 1109.7 %all-gather.11.cloned.1.call-start = ((), (), s32[]{:S(2)}) async-start(), calls=%async_computation.1 | async-start | bytes 1327104 | tf_op jit(solution)/shard_map/all_gather | solution.py:88
  8.7 1113.3 %all-gather.13.cloned.1.call-start = ((), (), s32[]{:S(2)}) async-start(), calls=%async_computation.2 | async-start | bytes 5308416 | tf_op jit(solution)/shard_map/all_gather | solution.py:92
  9.4 1151.3 %all-gather.15.cloned.1.call-start = ((), (), s32[]{:S(2)}) async-start(), calls=%async_computation.3 | async-start | bytes 5308416 | tf_op jit(solution)/shard_map/all_gather | solution.py:94
  10.0 3052.2 %all-gather.17.cloned.1.call-start = ((), (), s32[]{:S(2)}) async-start(), calls=%async_computation.4 | async-start | bytes 17717760 | tf_op jit(solution)/shard_map/all_gather | solution.py:270
  11.9 832.0 %copy-start.2 = (s32[12,1024,1]{1,2,0:T(1,128)}, s32[12,1024,1]{1,2,0:T(1,128)S(1)}, u32[]{:S(2)}) copy-start(s32[12,1024,1]{1,2,0:T(1,128)S(1)} %get-tuple-element.110) | copy-start | bytes 147460
  13.8 97.3 %copy-start.49 = (s32[1,1024]{1,0:T(1,128)S(1)}, s32[1,1024]{1,0:T(1,128)}, u32[]{:S(2)}) copy-start(s32[1,1024]{1,0:T(1,128)} %param.39) | copy-start | bytes 12292
  305.6 97.5 %copy-start.30 = (s32[1,12,1024]{2,0,1:T(1,128)S(1)}, s32[1,12,1024]{2,0,1:T(1,128)}, u32[]{:S(2)}) copy-start(s32[1,12,1024]{2,0,1:T(1,128)} %param.41) | copy-start | bytes 147460
  305.6 97.6 %copy-start.31 = (s32[1,12,1024]{2,0,1:T(1,128)S(1)}, s32[1,12,1024]{2,0,1:T(1,128)}, u32[]{:S(2)}) copy-start(s32[1,12,1024]{2,0,1:T(1,128)} %param.42) | copy-start | bytes 147460
  305.6 97.8 %copy-start.54 = (s32[3]{0:T(128)S(1)}, s32[3]{0:T(128)}, u32[]{:S(2)}) copy-start(s32[3]{0:T(128)} %constant.127) | copy-start | bytes 40
  305.6 98.4 %copy-start.53 = (s32[3]{0:T(128)S(1)}, s32[3]{0:T(128)}, u32[]{:S(2)}) copy-start(s32[3]{0:T(128)} %constant.130) | copy-start | bytes 40
  305.6 190.7 %copy-start.52 = (bf16[384]{0:T(512)(128)(2,1)S(1)}, bf16[384]{0:T(512)(128)(2,1)}, u32[]{:S(2)}) copy-start(bf16[384]{0:T(512)(128)(2,1)} %param.34) | copy-start | bytes 2308
  305.7 190.8 %copy-start.51 = (u32[32]{0:T(128)S(1)}, u32[32]{0:T(128)}, u32[]{:S(2)}) copy-start(u32[32]{0:T(128)} %constant.302) | copy-start | bytes 388
  305.7 192.0 %copy-start.56 = (bf16[96]{0:T(256)(128)(2,1)S(1)}, bf16[96]{0:T(256)(128)(2,1)}, u32[]{:S(2)}) copy-start(bf16[96]{0:T(256)(128)(2,1)} %param.37) | copy-start | bytes 580
  305.7 192.2 %copy-start.57 = (bf16[96]{0:T(256)(128)(2,1)S(1)}, bf16[96]{0:T(256)(128)(2,1)}, u32[]{:S(2)}) copy-start(bf16[96]{0:T(256)(128)(2,1)} %param.36) | copy-start | bytes 580
  305.7 192.5 %copy-start.58 = (bf16[96]{0:T(256)(128)(2,1)S(1)}, bf16[96]{0:T(256)(128)(2,1)}, u32[]{:S(2)}) copy-start(bf16[96]{0:T(256)(128)(2,1)} %param.31) | copy-start | bytes 580
  305.7 192.7 %copy-start.59 = (bf16[96]{0:T(256)(128)(2,1)S(1)}, bf16[96]{0:T(256)(128)(2,1)}, u32[]{:S(2)}) copy-start(bf16[96]{0:T(256)(128)(2,1)} %param.32) | copy-start | bytes 580
  305.7 192.9 %copy-start.60 = (bf16[96]{0:T(256)(128)(2,1)S(1)}, bf16[96]{0:T(256)(128)(2,1)}, u32[]{:S(2)}) copy-start(bf16[96]{0:T(256)(128)(2,1)} %param.30) | copy-start | bytes 580
  305.7 193.1 %copy-start.61 = (bf16[96]{0:T(256)(128)(2,1)S(1)}, bf16[96]{0:T(256)(128)(2,1)}, u32[]{:S(2)}) copy-start(bf16[96]{0:T(256)(128)(2,1)} %param.28) | copy-start | bytes 580
  305.7 193.4 %copy-start.62 = (bf16[96]{0:T(256)(128)(2,1)S(1)}, bf16[96]{0:T(256)(128)(2,1)}, u32[]{:S(2)}) copy-start(bf16[96]{0:T(256)(128)(2,1)} %param.27) | copy-start | bytes 580
  305.8 193.6 %copy-start.63 = (bf16[96]{0:T(256)(128)(2,1)S(1)}, bf16[96]{0:T(256)(128)(2,1)}, u32[]{:S(2)}) copy-start(bf16[96]{0:T(256)(128)(2,1)} %param.38) | copy-start | bytes 580
  403.0 164.4 %copy-start.25 = (bf16[1,1024,768]{2,1,0:T(8,128)(2,1)S(1)}, bf16[1,1024,768]{2,1,0:T(8,128)(2,1)}, u32[]{:S(2)}) copy-start(bf16[1,1024,768]{2,1,0:T(8,128)(2,1)} %param.43) | copy-start | bytes 4718596
  403.2 581.9 %copy-start.32 = (s32[1,12,1024]{2,0,1:T(1,128)}, s32[1,12,1024]{2,0,1:T(1,128)S(1)}, u32[]{:S(2)}) copy-start(s32[1,12,1024]{2,0,1:T(1,128)S(1)} %get-tuple-element.108) | copy-start | bytes 147460
  403.4 581.7 %copy-start.34 = (s32[1,12,1024]{2,0,1:T(1,128)}, s32[1,12,1024]{2,0,1:T(1,128)S(1)}, u32[]{:S(2)}) copy-start(s32[1,12,1024]{2,0,1:T(1,128)S(1)} %get-tuple-element.106) | copy-start | bytes 147460
  496.3 619.7 %copy-start.37 = (pred[12,1024]{1,0:T(8,128)(4,1)}, pred[12,1024]{1,0:T(8,128)(4,1)S(1)}, u32[]{:S(2)}) copy-start(pred[12,1024]{1,0:T(8,128)(4,1)S(1)} %and_bitcast_fusion.1) | copy-start | bytes 36868
  566.1 400.4 %copy-start.39 = (pred[1,12,1024,1]{2,1,3,0:T(8,128)(4,1)}, pred[1,12,1024,1]{2,1,3,0:T(8,128)(4,1)S(1)}, u32[]{:S(2)}) copy-start(pred[1,12,1024,1]{2,1,3,0:T(8,128)(4,1)S(1)} %copy.184) | copy-start | bytes 36868
  566.4 418.6 %copy-start.41 = (pred[12,8,128]{2,1,0:T(8,128)(4,1)}, pred[12,8,128]{2,1,0:T(8,128)(4,1)S(1)}, u32[]{:S(2)}) copy-start(pred[12,8,128]{2,1,0:T(8,128)(4,1)S(1)} %slice.147) | copy-start | bytes 36868
  566.7 418.4 %copy-start.43 = (pred[12,8,128]{2,1,0:T(8,128)(4,1)}, pred[12,8,128]{2,1,0:T(8,128)(4,1)S(1)}, u32[]{:S(2)}) copy-start(pred[12,8,128]{2,1,0:T(8,128)(4,1)S(1)} %slice.148) | copy-start | bytes 36868
  567.4 426.0 %copy-start.5 = (s32[12288]{0:T(1024)}, s32[12288]{0:T(1024)S(1)}, u32[]{:S(2)}) copy-start(s32[12288]{0:T(1024)S(1)} %reshape.757) | copy-start | bytes 147460
  568.6 9.5 copy-start.8
  967.2 12.3 copy-start.19
  979.5 13.8 copy-start.7
  979.6 5.5 copy-start.27
  1121.5 39.2 %copy-start.10 = (f32[1024,768]{0,1:T(8,128)}, f32[1024,768]{0,1:T(8,128)S(1)}, u32[]{:S(2)}) copy-start(f32[1024,768]{0,1:T(8,128)S(1)} %get-tuple-element.122) | copy-start | bytes 9437188
  1122.0 38.7 %copy-start.50 = (f32[768]{0:T(1024)S(1)}, f32[768]{0:T(1024)}, u32[]{:S(2)}) copy-start(f32[768]{0:T(1024)} %convert_element_type.140) | copy-start | bytes 9220
  1160.7 10.2 copy-start.9
  1160.7 10.2 copy-start.46
  1199.9 10.6 copy-start.11
  1199.9 10.6 copy-start.64
  1352.0 8.9 slice-start
  1352.7 8.2 slice-start.1
  1352.7 8.2 copy-start.28
  1790.8 9.3 copy-start.21
  1815.3 8.4 copy-start.12
  1863.2 28.9 copy-start.48
  2962.6 9.0 copy-start.16
  3132.8 17.8 copy-start.1
  (26 other events, 85.5 us)
Sparse Core Ops, SparseCore 0:
  10.2 67.8 all-gather.8
  80.3 39.5 all-gather.10
  122.1 78.6 all-gather.12
  202.8 78.0 all-gather.14
  2971.7 90.5 all-gather.16
